TPU v7x, 32 devices: a whole 2x2x4 slice. The times are simulated.
32 devices in a mesh: expert: 4 (over z), dp: 4 (over y, core), replica: 2 (over x).
Axes of the slice: x: 2, y: 2, z: 4, core: 2. Of those that a mesh axis runs over, the one named last changes fastest.
Arguments:
- cotangent: bfloat16 [2, 4, 4, 128, 2048], P('replica', 'expert', 'dp'), may hold values from -0.5 to 0.5
- expert_ids: int32 [2, 4, 4, 128, 2], P('replica', 'expert', 'dp'), may hold values from 0 to 3, all different within a row; in each aligned block of 128 rows (0 to 127, 128 to 255, ..., all dimensions but the last counted through in order) at most 96 rows name the same one
- gate_values: float32 [2, 4, 4, 128, 2], P('replica', 'expert', 'dp'), may hold values from 0.1 to 1
- hidden_saved: bfloat16 [2, 4, 4, 4, 4, 24, 7168], P('replica', 'expert', 'dp'), may hold values from -6 to 6
- output_saved: bfloat16 [2, 4, 4, 4, 4, 24, 2048], P('replica', 'expert', 'dp'), may hold values from -6 to 6
- weights: bfloat16 [2, 4, 7168, 2048], P('replica', 'expert', 'dp'), may hold values from -6 to 6
- moment_one: bfloat16 [2, 4, 7168, 2048], P('replica', 'expert', 'dp'), may hold values from -4 to 4
- moment_two: bfloat16 [2, 4, 7168, 2048], P('replica', 'expert', 'dp'), may hold values from 0.19921875 to 2
- anchor: float32 [4, 1792, 2048], P('expert', 'dp'), may hold values from -6 to 6
- outer_moment: float32 [4, 1792, 2048], P('expert', 'dp'), may hold values from -2 to 2
Outputs:
- new_weights: bfloat16 [2, 4, 7168, 2048], P('replica', 'expert', 'dp')
- gate_grads: float32 [2, 4, 4, 128, 2], P('replica', 'expert', 'dp')
- grad_rms: float32 [2], P('replica')
Inputs may be any that keep to these rules, and one draw needn't show every extreme that they name: `expert_ids`: each token names two different experts; among the 128 tokens of one device no expert is named more than 96 times, a bound that some block reaches.
All inputs are finite; a program needn't handle non-finite values.
Results may differ from a plain program's by a relative error of at most 0.0075.
Values may be sent and summed in bfloat16 or wider, within the bound.
A program may use at most 192 MiB of HBM per device.

v0:
```python
import jax
import jax.numpy as jnp
from jax import lax
from jax.sharding import PartitionSpec as P

beta_one = 0.9
beta_two = 0.95
epsilon = 1e-08
inner_rate = 0.3
weight_decay = 0.1
outer_rate = 0.7
nesterov_coef = 0.9


def shards(
    cotangent,
    expert_ids,
    gate_values,
    hidden_saved,
    output_saved,
    weights,
    moment_one,
    moment_two,
    anchor,
    outer_moment,
):
    n_exp = lax.axis_size("expert")
    n_dp = lax.axis_size("dp")
    n_rep = lax.axis_size("replica")
    tok_rows = cotangent.shape[3]
    model_width = cotangent.shape[4]
    capacity = hidden_saved.shape[5]
    hidden_width = hidden_saved.shape[6]
    slots_dev = n_exp * n_dp * capacity
    shard_rows = hidden_width // n_dp
    chosen = expert_ids.reshape(-1)
    onehot = (chosen[:, None] == jnp.arange(n_exp, dtype=jnp.int32)[None, :]).astype(jnp.int32)
    before = jnp.cumsum(onehot, axis=0) - onehot
    order_rank = jnp.sum(before * onehot, axis=1)
    position = (chosen * n_dp + order_rank % n_dp) * capacity + order_rank // n_dp
    stored = output_saved.reshape(n_exp, n_dp, capacity, model_width)
    returned = lax.all_to_all(
        stored.reshape(n_exp * n_dp, capacity, model_width),
        ("expert", "dp"),
        split_axis=0,
        concat_axis=0,
        tiled=True,
    )
    picked = jnp.take(returned.reshape(slots_dev, model_width), position, axis=0).reshape(
        tok_rows, 2, model_width
    )
    upstream = cotangent.reshape(tok_rows, model_width)
    gate_grads = jnp.einsum("tkd,td->tk", picked, upstream, preferred_element_type=jnp.float32)
    gates = gate_values.reshape(tok_rows, 2)
    sends = (gates[:, :, None] * upstream[:, None, :].astype(jnp.float32)).astype(jnp.bfloat16)
    buffer = (
        jnp.zeros((slots_dev, model_width), jnp.bfloat16)
        .at[position]
        .set(sends.reshape(2 * tok_rows, model_width))
    )
    arrived = lax.all_to_all(
        buffer.reshape(n_exp * n_dp, capacity, model_width),
        ("expert", "dp"),
        split_axis=0,
        concat_axis=0,
        tiled=True,
    )
    arrived = arrived.reshape(slots_dev, model_width)
    hidden = hidden_saved.reshape(slots_dev, hidden_width)
    gradient = lax.psum_scatter(
        lax.dot_general(
            hidden, arrived, (((0,), (0,)), ((), ())), preferred_element_type=jnp.float32
        ).astype(jnp.bfloat16),
        "dp",
        scatter_dimension=0,
        tiled=True,
    ).astype(jnp.float32)
    squares = lax.psum(jnp.sum(gradient * gradient), ("expert", "dp"))
    grad_rms = jnp.sqrt(squares / (n_exp * hidden_width * model_width)).reshape(1)
    weight_old = weights.reshape(shard_rows, model_width).astype(jnp.float32)
    first_new = (
        beta_one * moment_one.reshape(shard_rows, model_width).astype(jnp.float32)
        + (1.0 - beta_one) * gradient
    )
    second_new = (
        beta_two * moment_two.reshape(shard_rows, model_width).astype(jnp.float32)
        + (1.0 - beta_two) * gradient * gradient
    )
    inner_new = weight_old - inner_rate * (
        first_new / (jnp.sqrt(second_new) + epsilon) + weight_decay * weight_old
    )
    inner_new = inner_new.astype(jnp.bfloat16)
    grouped = inner_new.reshape(shard_rows // 4, 4, model_width)
    fragment = grouped[:, 0, :].astype(jnp.float32)
    start_point = anchor.reshape(shard_rows // 4, model_width)
    summed = lax.psum((start_point - fragment).astype(jnp.bfloat16), "replica").astype(jnp.float32)
    average = summed / n_rep
    momentum = nesterov_coef * outer_moment.reshape(shard_rows // 4, model_width) + average
    new_anchor = start_point - outer_rate * (average + nesterov_coef * momentum)
    updated = (
        grouped.at[:, 0, :]
        .set(new_anchor.astype(jnp.bfloat16))
        .reshape(1, 1, shard_rows, model_width)
    )
    return (updated, gate_grads.reshape(1, 1, 1, tok_rows, 2), grad_rms)


def solution(mesh):
    return jax.shard_map(
        shards,
        mesh=mesh,
        in_specs=(
            P("replica", "expert", "dp", None, None),
            P("replica", "expert", "dp", None, None),
            P("replica", "expert", "dp", None, None),
            P("replica", "expert", "dp", None, None, None, None),
            P("replica", "expert", "dp", None, None, None, None),
            P("replica", "expert", "dp", None),
            P("replica", "expert", "dp", None),
            P("replica", "expert", "dp", None),
            P("expert", "dp", None),
            P("expert", "dp", None),
        ),
        out_specs=(
            P("replica", "expert", "dp", None),
            P("replica", "expert", "dp", None, None),
            P("replica"),
        ),
        check_vma=False,
    )
```

profile of v0, /device:TPU:0, one launch (start us, length us, event | category | flops | bytes accessed | tf_op | source)
XLA Modules:
  0.0 495.1 jit_solution(3797463655363721530)
XLA Ops:
  8.3 1.2 reduce-window.6
  11.2 2.5 mul.136
  13.7 2.7 mul.137
  16.7 3.5 scatter_custom_fusion
  20.2 43.5 %all_to_all.10 = bf16[16,24,2048]{2,1,0:T(8,128)(2,1)S(1)} all-to-all(bf16[16,24,2048]{2,1,0:T(8,128)(2,1)} %bitcast.83), channel_id=1, replica_groups=mesh['expert'=4,'dp'=4,'replica'=2] {'expert','dp'}, dimensions={0} | all-to-all | bytes 3145728 | tf_op jit(solution)/shard_map/all_to_all | solution.py:61
  63.7 21.7 %convert_bitcast_fusion = bf16[7168,2048]{0,1:T(8,128)(2,1)} fusion(bf16[384,2048]{1,0:T(8,128)(2,1)S(1)} %bitcast.85, bf16[384,7168]{1,0:T(8,128)(2,1)} %bitcast.92), kind=kOutput, calls=%fused_computation.2 | convolution fusion | flops 11288969216 | bytes 36438016 | tf_op jit(solution)/shard_map/dot_general | solution.py:71
  85.4 5.0 %all-to-all-start.1 = ((bf16[16,24,2048]{2,1,0:T(8,128)(2,1)}), bf16[16,24,2048]{2,1,0:T(8,128)(2,1)S(1)}, u32[]{:S(2)}, u32[]{:S(2)}) async-start(bf16[16,24,2048]{2,1,0:T(8,128)(2,1)} %bitcast.84), calls=%async_computation.2 | async-start | bytes 3145728 | tf_op jit(solution)/shard_map/all_to_all | solution.py:42
  90.7 10.7 %copy.33 = bf16[1,1,1792,2048]{2,3,1,0:T(8,128)(2,1)} copy(bf16[1,1,1792,2048]{3,2,1,0:T(8,128)(2,1)} %param.17) | data formatting | bytes 14680064 | tf_op args[5]
  101.4 11.0 %copy.34 = bf16[1,1,1792,2048]{2,3,1,0:T(8,128)(2,1)} copy(bf16[1,1,1792,2048]{3,2,1,0:T(8,128)(2,1)} %param.18) | data formatting | bytes 14680064 | tf_op args[6]
  112.4 10.8 %copy.41 = bf16[1,1,1792,2048]{2,3,1,0:T(8,128)(2,1)} copy(bf16[1,1,1792,2048]{3,2,1,0:T(8,128)(2,1)} %param.19) | data formatting | bytes 14680064 | tf_op args[7]
  123.2 170.8 %reduce-scatter.2.cloned.1.call-done = bf16[1792,2048]{0,1:T(8,128)(2,1)} async-done(((bf16[7168,2048]{0,1:T(8,128)(2,1)}), bf16[1792,2048]{0,1:T(8,128)(2,1)}) %reduce-scatter.2.cloned.1.call-update) | async-done | bytes 7340048 | tf_op jit(solution)/shard_map/reduce_scatter | solution.py:70
  294.0 18.8 %fusion.8 = (f32[]{:T(128)}, bf16[1792,2048]{0,1:T(8,128)(2,1)}) fusion(bf16[1792,2048]{0,1:T(8,128)(2,1)} %reduce-scatter.2.cloned.1.call-done, bf16[1,1,1792,2048]{2,3,1,0:T(8,128)(2,1)} %copy.41, bf16[1,1,1792,2048]{2,3,1,0:T(8,128)(2,1)} %copy.34, bf16[1,1,1792,2048]{2,3,1,0:T(8,128)(2,1)} %copy.33), kind=kLoop, calls=%fused_computation.17 | loop fusion | flops 73400320 | bytes 36700164 | tf_op jit(solution)/shard_map/reduce_sum | solution.py:78
  312.7 10.2 %copy.42 = bf16[1792,2048]{1,0:T(8,128)(2,1)} copy(bf16[1792,2048]{0,1:T(8,128)(2,1)} %get-tuple-element.16) | data formatting | bytes 14680064 | tf_op jit(solution)/shard_map/convert_element_type | solution.py:92
  322.9 11.6 %reshape.232 = bf16[448,4,2048]{2,1,0:T(4,128)(2,1)} reshape(bf16[1792,2048]{1,0:T(8,128)(2,1)} %copy.42) | data formatting | bytes 14680064 | tf_op jit(solution)/shard_map/reshape | solution.py:93
  334.5 8.0 %slice_convert_fusion = f32[448,1,2048]{2,1,0:T(1,128)} fusion(bf16[448,4,2048]{2,1,0:T(4,128)(2,1)} %reshape.232), kind=kLoop, calls=%fused_computation.18 | loop fusion | flops 917504 | bytes 5505024 | tf_op jit(solution)/shard_map/convert_element_type | solution.py:94
  342.5 5.6 %fusion.9 = bf16[448,2048]{1,0:T(8,128)(2,1)} fusion(f32[448,1,2048]{2,1,0:T(1,128)} %slice_convert_fusion, f32[1,448,2048]{2,1,0:T(8,128)} %param.20), kind=kLoop, calls=%fused_computation.20 | loop fusion | flops 1835008 | bytes 9175040 | tf_op jit(solution)/shard_map/convert_element_type | solution.py:96
  348.4 1.4 gather_fusion
  350.5 3.8 fusion.18
  355.0 32.8 %psum.15 = f32[]{:T(128)} all-reduce(f32[]{:T(128)} %get-tuple-element.15), channel_id=1, replica_groups=mesh['expert'=4,'dp'=4,'replica'=2] {'expert','dp'}, use_global_device_ids=true, to_apply=%region_7.8 | all-reduce | flops 1 | bytes 8 | tf_op jit(solution)/shard_map/psum | solution.py:78
  388.5 17.1 %all-reduce.2.cloned.1.call-done = bf16[448,2048]{1,0:T(8,128)(2,1)} async-done(((bf16[448,2048]{1,0:T(8,128)(2,1)}), bf16[448,2048]{1,0:T(8,128)(2,1)}) %all-reduce.2.cloned.1.call-update) | async-done | bytes 1835024 | tf_op jit(solution)/shard_map/psum | solution.py:96
  405.6 4.8 fusion.15
  410.4 4.7 copy.43
  415.1 61.0 %scatter.13 = bf16[448,4,2048]{2,1,0:T(4,128)(2,1)} dynamic-update-slice(bf16[448,4,2048]{2,1,0:T(4,128)(2,1)} %reshape.232, bf16[448,1,2048]{2,1,0:T(2,128)(2,1)} %copy.43, s32[]{:T(128)} %constant.88.clone.1, s32[]{:T(128)} %constant.88.clone.1, s32[]{:T(128)} %constant.88.clone.1) | dynamic-update-slice | bytes 3670020 | tf_op jit(solution)/shard_map/scatter | solution.py:102
  476.1 11.0 %reshape.235 = bf16[1,1,1792,2048]{3,2,1,0:T(8,128)(2,1)} reshape(bf16[448,4,2048]{2,1,0:T(4,128)(2,1)} %scatter.13) | data formatting | bytes 14680064 | tf_op jit(solution)/shard_map/reshape | solution.py:103
  (31 shorter events, 4.9 us)
Async XLA Ops:
  7.2 9.3 %copy-start.1 = (f32[1,1,1,128,2]{3,4,2,1,0:T(2,128)S(1)}, f32[1,1,1,128,2]{3,4,2,1,0:T(2,128)}, u32[]{:S(2)}) copy-start(f32[1,1,1,128,2]{3,4,2,1,0:T(2,128)} %param.14) | copy-start | bytes 3076
  7.2 286.8 %reduce-scatter.2.cloned.1.call-start = ((), (), s32[]{:S(2)}) async-start(), calls=%async_computation.3 | async-start | bytes 36700160 | tf_op jit(solution)/shard_map/reduce_scatter | solution.py:70
  85.4 263.0 %all-to-all-start.1 = ((bf16[16,24,2048]{2,1,0:T(8,128)(2,1)}), bf16[16,24,2048]{2,1,0:T(8,128)(2,1)S(1)}, u32[]{:S(2)}, u32[]{:S(2)}) async-start(bf16[16,24,2048]{2,1,0:T(8,128)(2,1)} %bitcast.84), calls=%async_computation.2 | async-start | bytes 3145728 | tf_op jit(solution)/shard_map/all_to_all | solution.py:42
  90.5 315.1 %all-reduce.2.cloned.1.call-start = ((), (), s32[]{:S(2)}) async-start(), calls=%async_computation.4 | async-start | bytes 3670016 | tf_op jit(solution)/shard_map/psum | solution.py:96
  348.4 2.1 copy-start
Sparse Core Ops, SparseCore 0:
  85.5 208.3 reduce-scatter.1
  348.3 57.2 all-reduce.1
where the time goes:
time: 501 us; the launch traced here: 495 us
  waiting for transfers between devices  188 us (38%)
  local copies, waits for them, and re-layouts  141 us (28%)
  blocking collectives  76.3 us (15%)
  other arithmetic  43.3 us (9%)
  matrix products  25.4 us (5%)
  between operations  16 us (3%)
  starting transfers between devices  5.3 us (1%)
    reduce_scatter x1, waiting for transfers between devices, shards(): lax.psum_scatter(lax.dot_general(hidden, arrived, (((0,), (0,)), ((), ())...  171 us
    scatter x1, local copies, waits for them, and re-layouts, shards(): updated = grouped.at[:, 0, :].set(new_anchor.astype(jnp.bfloat16)).reshap...  61 us
    all_to_all x1, blocking collectives, shards(): lax.all_to_all(buffer.reshape(n_exp * n_dp, capacity, model_width), ('exp...  43.5 us
    unnamed x9, local copies, waits for them, and re-layouts  33.4 us
    psum x1, blocking collectives, shards(): squares = lax.psum(jnp.sum(gradient * gradient), ('expert', 'dp'))  32.8 us
    dot_general x1, matrix products, shards(): lax.dot_general(hidden, arrived, (((0,), (0,)), ((), ())), preferred_elem...  21.7 us
    reduce_sum x1, other arithmetic, shards(): squares = lax.psum(jnp.sum(gradient * gradient), ('expert', 'dp'))  18.8 us
    psum x1, waiting for transfers between devices, shards(): lax.psum((start_point - fragment).astype(jnp.bfloat16), 'replica')  17.1 us
  transfers between devices with their start and end apart: 3, of which 2 were waited for; matrix products, arithmetic and copies ran while one was open for 19% of the time, Pallas kernels for 0%

commit v1 on v0

--- a/solution.py
+++ b/solution.py
@@ -10,6 +10,18 @@
 weight_decay = 0.1
 outer_rate = 0.7
 nesterov_coef = 0.9
+
+
+def split_up(value, dim, count):
+    dims = value.shape
+    pieces = value.reshape(*dims[:dim], count, dims[dim] // count, *dims[dim + 1 :])
+    return jnp.moveaxis(pieces, dim, 0)
+
+
+def in_order(blocks, dim):
+    blocks = jnp.moveaxis(blocks, 0, dim)
+    dims = blocks.shape
+    return blocks.reshape(*dims[:dim], dims[dim] * dims[dim + 1], *dims[dim + 2 :])
 
 
 def shards(
@@ -58,13 +70,17 @@
         .at[position]
         .set(sends.reshape(2 * tok_rows, model_width))
     )
-    arrived = lax.all_to_all(
-        buffer.reshape(n_exp * n_dp, capacity, model_width),
-        ("expert", "dp"),
-        split_axis=0,
-        concat_axis=0,
-        tiled=True,
-    )
+    shard = buffer.reshape(n_exp * n_dp, capacity, model_width)
+    length, index = (lax.axis_size(("expert", "dp")), lax.axis_index(("expert", "dp")))
+    blocks = split_up(shard, 0, length)
+    outs = [blocks[index]]
+    for step in range(1, length):
+        sent = blocks[(index + step) % length]
+        outs.append(
+            lax.ppermute(sent, ("expert", "dp"), [(i, (i + step) % length) for i in range(length)])
+        )
+    blocks = jnp.stack(outs)[(index - jnp.arange(length)) % length]
+    arrived = in_order(blocks, 0)
     arrived = arrived.reshape(slots_dev, model_width)
     hidden = hidden_saved.reshape(slots_dev, hidden_width)
     gradient = lax.psum_scatter(

time: 501 us -> 507 us (1.012)
  blocking collectives: 76.3 us -> 32.9 us
  starting transfers between devices: 5.3 us -> 33.7 us
  waiting for transfers between devices: 188 us -> 203 us
    all_to_all x1 -> x0, blocking collectives: 43.5 us -> none  [shards(): lax.all_to_all(buffer.reshape(n_exp * n_dp, capacity, model_width), ('exp...]
    ppermute x0 -> x15, starting transfers between devices: none -> 27.4 us  [shards(): lax.ppermute(sent, ('expert', 'dp'), [(i, (i + step) % length) for i in r...]
    ppermute x0 -> x15, waiting for transfers between devices: none -> 15.4 us  [shards(): lax.ppermute(sent, ('expert', 'dp'), [(i, (i + step) % length) for i in r...]
    unnamed x9 -> x23, local copies, waits for them, and re-layouts: 33.4 us -> 33.7 us
  transfers between devices with their start and end apart: 3 -> 18, of which waited for: 2 -> 8; matrix products, arithmetic and copies ran while one was open for 19% -> 19% of each run, Pallas kernels for 0% -> 0%
where the time goes in v1:
time: 507 us; the launch traced here: 500 us
  waiting for transfers between devices  203 us (40%)
  local copies, waits for them, and re-layouts  145 us (29%)
  other arithmetic  43.3 us (9%)
  starting transfers between devices  33.7 us (7%)
  blocking collectives  32.9 us (6%)
  matrix products  25.9 us (5%)
  between operations  16.4 us (3%)
    reduce_scatter x1, waiting for transfers between devices, shards(): lax.psum_scatter(lax.dot_general(hidden, arrived, (((0,), (0,)), ((), ())...  171 us
    scatter x1, local copies, waits for them, and re-layouts, shards(): updated = grouped.at[:, 0, :].set(new_anchor.astype(jnp.bfloat16)).reshap...  61.3 us
    unnamed x23, local copies, waits for them, and re-layouts  33.7 us
    psum x1, blocking collectives, shards(): squares = lax.psum(jnp.sum(gradient * gradient), ('expert', 'dp'))  32.9 us
    ppermute x15, starting transfers between devices, shards(): lax.ppermute(sent, ('expert', 'dp'), [(i, (i + step) % length) for i in r...  27.4 us
    dot_general x1, matrix products, shards(): lax.dot_general(hidden, arrived, (((0,), (0,)), ((), ())), preferred_elem...  22.4 us
    reduce_sum x1, other arithmetic, shards(): squares = lax.psum(jnp.sum(gradient * gradient), ('expert', 'dp'))  18.8 us
    psum x1, waiting for transfers between devices, shards(): lax.psum((start_point - fragment).astype(jnp.bfloat16), 'replica')  17 us
  transfers between devices with their start and end apart: 18, of which 8 were waited for; matrix products, arithmetic and copies ran while one was open for 19% of the time, Pallas kernels for 0%

profile of v1, /device:TPU:0, one launch (start us, length us, event | category | flops | bytes accessed | tf_op | source)
XLA Modules:
  0.0 500.5 jit_solution(17669759072658775769)
XLA Ops:
  17.0 3.5 scatter_custom_fusion
  31.4 3.6 collective-permute-start.6
  36.7 11.0 %collective-permute-done.4 = bf16[1,24,2048]{2,1,0:T(8,128)(2,1)S(1)} collective-permute-done((bf16[1,24,2048]{2,1,0:T(8,128)(2,1)S(1)}, bf16[1,24,2048]{2,1,0:T(8,128)(2,1)S(1)}, u32[]{:S(2)}, u32[]{:S(2)}) %collective-permute-start.4) | collective-permute-done | bytes 98336 | tf_op jit(solution)/shard_map/ppermute | solution.py:80
  47.9 3.0 collective-permute-start.10
  50.9 4.3 collective-permute-start.11
  56.8 3.7 collective-permute-start.13
  67.0 22.4 %convert_bitcast_fusion = bf16[7168,2048]{0,1:T(8,128)(2,1)} fusion(bf16[384,2048]{1,0:T(8,128)(2,1)} %bitcast.149, bf16[384,7168]{1,0:T(8,128)(2,1)} %bitcast.156), kind=kOutput, calls=%fused_computation.3 | convolution fusion | flops 11288969216 | bytes 36438016 | tf_op jit(solution)/shard_map/dot_general | solution.py:87
  89.3 6.0 %all-to-all-start = ((bf16[16,24,2048]{2,1,0:T(8,128)(2,1)}), bf16[16,24,2048]{2,1,0:T(8,128)(2,1)S(1)}, u32[]{:S(2)}, u32[]{:S(2)}) async-start(bf16[16,24,2048]{2,1,0:T(8,128)(2,1)} %bitcast.148), calls=%async_computation.1 | async-start | bytes 3145728 | tf_op jit(solution)/shard_map/all_to_all | solution.py:54
  95.6 10.8 %copy.33 = bf16[1,1,1792,2048]{2,3,1,0:T(8,128)(2,1)} copy(bf16[1,1,1792,2048]{3,2,1,0:T(8,128)(2,1)} %param.17) | data formatting | bytes 14680064 | tf_op args[5]
  106.4 10.9 %copy.34 = bf16[1,1,1792,2048]{2,3,1,0:T(8,128)(2,1)} copy(bf16[1,1,1792,2048]{3,2,1,0:T(8,128)(2,1)} %param.18) | data formatting | bytes 14680064 | tf_op args[6]
  117.3 10.8 %copy.41 = bf16[1,1,1792,2048]{2,3,1,0:T(8,128)(2,1)} copy(bf16[1,1,1792,2048]{3,2,1,0:T(8,128)(2,1)} %param.19) | data formatting | bytes 14680064 | tf_op args[7]
  128.0 170.8 %reduce-scatter.2.cloned.1.call-done = bf16[1792,2048]{0,1:T(8,128)(2,1)} async-done(((bf16[7168,2048]{0,1:T(8,128)(2,1)}), bf16[1792,2048]{0,1:T(8,128)(2,1)}) %reduce-scatter.2.cloned.1.call-update) | async-done | bytes 7340048 | tf_op jit(solution)/shard_map/reduce_scatter | solution.py:86
  298.9 18.8 %fusion.8 = (f32[]{:T(128)}, bf16[1792,2048]{0,1:T(8,128)(2,1)}) fusion(bf16[1792,2048]{0,1:T(8,128)(2,1)} %reduce-scatter.2.cloned.1.call-done, bf16[1,1,1792,2048]{2,3,1,0:T(8,128)(2,1)} %copy.41, bf16[1,1,1792,2048]{2,3,1,0:T(8,128)(2,1)} %copy.34, bf16[1,1,1792,2048]{2,3,1,0:T(8,128)(2,1)} %copy.33), kind=kLoop, calls=%fused_computation.18 | loop fusion | flops 73400320 | bytes 36700164 | tf_op jit(solution)/shard_map/reduce_sum | solution.py:94
  317.6 10.4 %copy.42 = bf16[1792,2048]{1,0:T(8,128)(2,1)} copy(bf16[1792,2048]{0,1:T(8,128)(2,1)} %get-tuple-element.16) | data formatting | bytes 14680064 | tf_op jit(solution)/shard_map/convert_element_type | solution.py:108
  328.0 11.6 %reshape.273 = bf16[448,4,2048]{2,1,0:T(4,128)(2,1)} reshape(bf16[1792,2048]{1,0:T(8,128)(2,1)} %copy.42) | data formatting | bytes 14680064 | tf_op jit(solution)/shard_map/reshape | solution.py:109
  339.6 8.0 %slice_convert_fusion = f32[448,1,2048]{2,1,0:T(1,128)} fusion(bf16[448,4,2048]{2,1,0:T(4,128)(2,1)} %reshape.273), kind=kLoop, calls=%fused_computation.19 | loop fusion | flops 917504 | bytes 5505024 | tf_op jit(solution)/shard_map/convert_element_type | solution.py:110
  347.7 5.6 %fusion.9 = bf16[448,2048]{1,0:T(8,128)(2,1)} fusion(f32[448,1,2048]{2,1,0:T(1,128)} %slice_convert_fusion, f32[1,448,2048]{2,1,0:T(8,128)} %param.20), kind=kLoop, calls=%fused_computation.21 | loop fusion | flops 1835008 | bytes 9175040 | tf_op jit(solution)/shard_map/convert_element_type | solution.py:112
  356.0 3.5 fusion.18
  360.1 32.9 %psum.15 = f32[]{:T(128)} all-reduce(f32[]{:T(128)} %get-tuple-element.15), channel_id=1, replica_groups=mesh['expert'=4,'dp'=4,'replica'=2] {'expert','dp'}, use_global_device_ids=true, to_apply=%region_7.8 | all-reduce | flops 1 | bytes 8 | tf_op jit(solution)/shard_map/psum | solution.py:94
  393.7 17.0 %all-reduce.2.cloned.1.call-done = bf16[448,2048]{1,0:T(8,128)(2,1)} async-done(((bf16[448,2048]{1,0:T(8,128)(2,1)}), bf16[448,2048]{1,0:T(8,128)(2,1)}) %all-reduce.2.cloned.1.call-update) | async-done | bytes 1835024 | tf_op jit(solution)/shard_map/psum | solution.py:112
  410.7 4.8 fusion.15
  415.5 4.7 copy.43
  420.1 61.3 %scatter.13 = bf16[448,4,2048]{2,1,0:T(4,128)(2,1)} dynamic-update-slice(bf16[448,4,2048]{2,1,0:T(4,128)(2,1)} %reshape.273, bf16[448,1,2048]{2,1,0:T(2,128)(2,1)} %copy.43, s32[]{:T(128)} %constant.185.clone.1, s32[]{:T(128)} %constant.185.clone.1, s32[]{:T(128)} %constant.185.clone.1) | dynamic-update-slice | bytes 3670020 | tf_op jit(solution)/shard_map/scatter | solution.py:118
  481.5 11.0 %reshape.276 = bf16[1,1,1792,2048]{3,2,1,0:T(8,128)(2,1)} reshape(bf16[448,4,2048]{2,1,0:T(4,128)(2,1)} %scatter.13) | data formatting | bytes 14680064 | tf_op jit(solution)/shard_map/reshape | solution.py:119
  (79 shorter events, 33.8 us)
Async XLA Ops:
  7.2 291.7 %reduce-scatter.2.cloned.1.call-start = ((), (), s32[]{:S(2)}) async-start(), calls=%async_computation.2 | async-start | bytes 36700160 | tf_op jit(solution)/shard_map/reduce_scatter | solution.py:86
  13.9 2.7 copy-start.1
  22.1 7.9 %collective-permute-start = (bf16[1,24,2048]{2,1,0:T(8,128)(2,1)S(1)}, bf16[1,24,2048]{2,1,0:T(8,128)(2,1)S(1)}, u32[]{:S(2)}, u32[]{:S(2)}) collective-permute-start(bf16[1,24,2048]{2,1,0:T(8,128)(2,1)S(1)} %get-tuple-element.31), channel_id=1, source_target_pairs={{0,2},{2,4},{4,6},{6,8},{8,10},{10,12},{12,14},{14,16},{16,18},{18... | collective-permute-start | bytes 294920 | tf_op jit(solution)/shard_map/ppermute | solution.py:80
  22.6 8.8 %collective-permute-start.1 = (bf16[1,24,2048]{2,1,0:T(8,128)(2,1)S(1)}, bf16[1,24,2048]{2,1,0:T(8,128)(2,1)S(1)}, u32[]{:S(2)}, u32[]{:S(2)}) collective-permute-start(bf16[1,24,2048]{2,1,0:T(8,128)(2,1)S(1)} %get-tuple-element.30), channel_id=1, source_target_pairs={{0,4},{2,6},{4,8},{6,10},{8,12},{10,14},{12,16},{14,18},{16,20},{1... | collective-permute-start | bytes 294920 | tf_op jit(solution)/shard_map/ppermute | solution.py:80
  25.2 9.8 %collective-permute-start.2 = (bf16[1,24,2048]{2,1,0:T(8,128)(2,1)S(1)}, bf16[1,24,2048]{2,1,0:T(8,128)(2,1)S(1)}, u32[]{:S(2)}, u32[]{:S(2)}) collective-permute-start(bf16[1,24,2048]{2,1,0:T(8,128)(2,1)S(1)} %get-tuple-element.29), channel_id=1, source_target_pairs={{0,6},{2,8},{4,10},{6,12},{8,14},{10,16},{12,18},{14,20},{16,22},{... | collective-permute-start | bytes 294920 | tf_op jit(solution)/shard_map/ppermute | solution.py:80
  27.6 7.8 %collective-permute-start.3 = (bf16[1,24,2048]{2,1,0:T(8,128)(2,1)S(1)}, bf16[1,24,2048]{2,1,0:T(8,128)(2,1)S(1)}, u32[]{:S(2)}, u32[]{:S(2)}) collective-permute-start(bf16[1,24,2048]{2,1,0:T(8,128)(2,1)S(1)} %get-tuple-element.28), channel_id=1, source_target_pairs={{0,8},{2,10},{4,12},{6,14},{8,16},{10,18},{12,20},{14,22},{16,24},... | collective-permute-start | bytes 294920 | tf_op jit(solution)/shard_map/ppermute | solution.py:80
  29.2 18.5 %collective-permute-start.4 = (bf16[1,24,2048]{2,1,0:T(8,128)(2,1)S(1)}, bf16[1,24,2048]{2,1,0:T(8,128)(2,1)S(1)}, u32[]{:S(2)}, u32[]{:S(2)}) collective-permute-start(bf16[1,24,2048]{2,1,0:T(8,128)(2,1)S(1)} %get-tuple-element.27), channel_id=1, source_target_pairs={{0,10},{2,12},{4,14},{6,16},{8,18},{10,20},{12,22},{14,24},{16,26}... | collective-permute-start | bytes 294920 | tf_op jit(solution)/shard_map/ppermute | solution.py:80
  30.1 17.9 %collective-permute-start.5 = (bf16[1,24,2048]{2,1,0:T(8,128)(2,1)S(1)}, bf16[1,24,2048]{2,1,0:T(8,128)(2,1)S(1)}, u32[]{:S(2)}, u32[]{:S(2)}) collective-permute-start(bf16[1,24,2048]{2,1,0:T(8,128)(2,1)S(1)} %get-tuple-element.26), channel_id=1, source_target_pairs={{0,12},{2,14},{4,16},{6,18},{8,20},{10,22},{12,24},{14,26},{16,28}... | collective-permute-start | bytes 294920 | tf_op jit(solution)/shard_map/ppermute | solution.py:80
  31.4 19.5 %collective-permute-start.6 = (bf16[1,24,2048]{2,1,0:T(8,128)(2,1)S(1)}, bf16[1,24,2048]{2,1,0:T(8,128)(2,1)S(1)}, u32[]{:S(2)}, u32[]{:S(2)}) collective-permute-start(bf16[1,24,2048]{2,1,0:T(8,128)(2,1)S(1)} %get-tuple-element.25), channel_id=1, source_target_pairs={{0,14},{2,16},{4,18},{6,20},{8,22},{10,24},{12,26},{14,28},{16,30}... | collective-permute-start | bytes 294920 | tf_op jit(solution)/shard_map/ppermute | solution.py:80
  35.0 20.2 %collective-permute-start.7 = (bf16[1,24,2048]{2,1,0:T(8,128)(2,1)S(1)}, bf16[1,24,2048]{2,1,0:T(8,128)(2,1)S(1)}, u32[]{:S(2)}, u32[]{:S(2)}) collective-permute-start(bf16[1,24,2048]{2,1,0:T(8,128)(2,1)S(1)} %get-tuple-element.24), channel_id=1, source_target_pairs={{0,16},{2,18},{4,20},{6,22},{8,24},{10,26},{12,28},{14,30},{16,0},... | collective-permute-start | bytes 294920 | tf_op jit(solution)/shard_map/ppermute | solution.py:80
  35.5 21.3 %collective-permute-start.8 = (bf16[1,24,2048]{2,1,0:T(8,128)(2,1)S(1)}, bf16[1,24,2048]{2,1,0:T(8,128)(2,1)S(1)}, u32[]{:S(2)}, u32[]{:S(2)}) collective-permute-start(bf16[1,24,2048]{2,1,0:T(8,128)(2,1)S(1)} %get-tuple-element.23), channel_id=1, source_target_pairs={{0,18},{2,20},{4,22},{6,24},{8,26},{10,28},{12,30},{14,0},{16,2},{... | collective-permute-start | bytes 294920 | tf_op jit(solution)/shard_map/ppermute | solution.py:80
  47.7 12.8 %collective-permute-start.9 = (bf16[1,24,2048]{2,1,0:T(8,128)(2,1)S(1)}, bf16[1,24,2048]{2,1,0:T(8,128)(2,1)S(1)}, u32[]{:S(2)}, u32[]{:S(2)}) collective-permute-start(bf16[1,24,2048]{2,1,0:T(8,128)(2,1)S(1)} %get-tuple-element.22), channel_id=1, source_target_pairs={{0,20},{2,22},{4,24},{6,26},{8,28},{10,30},{12,0},{14,2},{16,4},{1... | collective-permute-start | bytes 294920 | tf_op jit(solution)/shard_map/ppermute | solution.py:80
  47.9 14.4 %collective-permute-start.10 = (bf16[1,24,2048]{2,1,0:T(8,128)(2,1)S(1)}, bf16[1,24,2048]{2,1,0:T(8,128)(2,1)S(1)}, u32[]{:S(2)}, u32[]{:S(2)}) collective-permute-start(bf16[1,24,2048]{2,1,0:T(8,128)(2,1)S(1)} %get-tuple-element.21), channel_id=1, source_target_pairs={{0,22},{2,24},{4,26},{6,28},{8,30},{10,0},{12,2},{14,4},{16,6},{18... | collective-permute-start | bytes 294920 | tf_op jit(solution)/shard_map/ppermute | solution.py:80
  50.9 11.4 %collective-permute-start.11 = (bf16[1,24,2048]{2,1,0:T(8,128)(2,1)S(1)}, bf16[1,24,2048]{2,1,0:T(8,128)(2,1)S(1)}, u32[]{:S(2)}, u32[]{:S(2)}) collective-permute-start(bf16[1,24,2048]{2,1,0:T(8,128)(2,1)S(1)} %get-tuple-element.20), channel_id=1, source_target_pairs={{0,24},{2,26},{4,28},{6,30},{8,0},{10,2},{12,4},{14,6},{16,8},{18,... | collective-permute-start | bytes 294920 | tf_op jit(solution)/shard_map/ppermute | solution.py:80
  55.3 7.1 %collective-permute-start.12 = (bf16[1,24,2048]{2,1,0:T(8,128)(2,1)S(1)}, bf16[1,24,2048]{2,1,0:T(8,128)(2,1)S(1)}, u32[]{:S(2)}, u32[]{:S(2)}) collective-permute-start(bf16[1,24,2048]{2,1,0:T(8,128)(2,1)S(1)} %get-tuple-element.19), channel_id=1, source_target_pairs={{0,26},{2,28},{4,30},{6,0},{8,2},{10,4},{12,6},{14,8},{16,10},{18,... | collective-permute-start | bytes 294920 | tf_op jit(solution)/shard_map/ppermute | solution.py:80
  56.8 6.8 %collective-permute-start.13 = (bf16[1,24,2048]{2,1,0:T(8,128)(2,1)S(1)}, bf16[1,24,2048]{2,1,0:T(8,128)(2,1)S(1)}, u32[]{:S(2)}, u32[]{:S(2)}) collective-permute-start(bf16[1,24,2048]{2,1,0:T(8,128)(2,1)S(1)} %get-tuple-element.18), channel_id=1, source_target_pairs={{0,28},{2,30},{4,0},{6,2},{8,4},{10,6},{12,8},{14,10},{16,12},{18,... | collective-permute-start | bytes 294920 | tf_op jit(solution)/shard_map/ppermute | solution.py:80
  60.5 4.6 collective-permute-start.14
  89.3 264.2 %all-to-all-start = ((bf16[16,24,2048]{2,1,0:T(8,128)(2,1)}), bf16[16,24,2048]{2,1,0:T(8,128)(2,1)S(1)}, u32[]{:S(2)}, u32[]{:S(2)}) async-start(bf16[16,24,2048]{2,1,0:T(8,128)(2,1)} %bitcast.148), calls=%async_computation.1 | async-start | bytes 3145728 | tf_op jit(solution)/shard_map/all_to_all | solution.py:54
  95.4 315.3 %all-reduce.2.cloned.1.call-start = ((), (), s32[]{:S(2)}) async-start(), calls=%async_computation.3 | async-start | bytes 3670016 | tf_op jit(solution)/shard_map/psum | solution.py:112
  354.9 1.0 copy-start
Sparse Core Ops, SparseCore 0:
  89.5 209.3 reduce-scatter.1
  353.4 57.2 all-reduce.1
